TPU v7x, 256 devices: a whole 4x4x8 slice. The times are simulated.
256 devices in a mesh: ctx: 32 (over z, x), ch: 8 (over y, core).
Axes of the slice: x: 4, y: 4, z: 8, core: 2. Of those that a mesh axis runs over, the one named last changes fastest.
Arguments:
- query_input: bfloat16 [4096, 4096], P('ctx', 'ch'), may hold values from -6 to 6
- key_input: bfloat16 [4096, 4096], P('ctx', 'ch'), may hold values from -6 to 6
- value_input: bfloat16 [4096, 4096], P('ctx', 'ch'), may hold values from -6 to 6
- short_weight: float32 [3, 3, 4096], P(None, None, 'ch'), may hold values from -3.5 to 3.5
- residue: float32 [16, 4096], P(None, 'ch'), may hold values from -1.5 to 1.5
- decay_rate: float32 [16, 4096], P(None, 'ch'), may hold values from 0.00012207031 to 0.05
- skip_gain: float32 [4096], P('ch'), may hold values from -1 to 1
- out_weight: bfloat16 [4096, 8192], P('ch'), may hold values from -0.125 to 0.125
Outputs:
- layer_output: bfloat16 [4096, 8192], P('ctx', 'ch')
All inputs are finite; a program needn't handle non-finite values.
Results may differ from a plain program's by a relative error of at most 0.015.
Values may be sent and summed in bfloat16 or wider, within the bound.
No kernel may reach another device: no remote copies, remote signals or barrier semaphores. Data moves between devices by JAX's collectives and lax.ppermute only.
A program may use at most 64 MiB of HBM per device.

v0:
```python
import math

import jax
import jax.numpy as jnp
import numpy as np
from jax import lax
from jax.sharding import PartitionSpec as P

HIGHEST = lax.Precision.HIGHEST


def swapped(value, axis, apart):
    mask = 2**apart
    pairs = [(source, source ^ mask) for source in range(lax.axis_size(axis))]
    return lax.ppermute(value, axis, pairs)


def passed_along(block, axis, distance):
    devices = range(lax.axis_size(axis))
    route = [(i - distance, i) for i in devices if i - distance in devices]
    return lax.ppermute(block, axis, route)


def short_filter(raw_rows, prior_rows, taps):
    extended = jnp.concatenate([prior_rows, raw_rows], axis=0).astype(jnp.float32)
    length_rows = raw_rows.shape[0]
    tap_count = taps.shape[0]
    running = jnp.zeros(raw_rows.shape, jnp.float32)
    for offset in range(tap_count):
        running = (
            running
            + taps[offset] * extended[tap_count - 1 - offset : tap_count - 1 - offset + length_rows]
        )
    return running


def reversed_index(device_index, bit_total):
    running = jnp.zeros((), jnp.int32)
    for position in range(bit_total):
        running = running + (device_index >> position & 1) * (1 << bit_total - 1 - position)
    return running


def local_matrix(row_count, sign_value):
    products = np.outer(np.arange(row_count), np.arange(row_count)) % row_count
    phases = sign_value * 2.0 * math.pi * products / row_count
    return (jnp.asarray(np.cos(phases), jnp.float32), jnp.asarray(np.sin(phases), jnp.float32))


def across_rows(real_part, imag_part, sign_value):
    mat_real, mat_imag = local_matrix(real_part.shape[1], sign_value)
    out_real = jnp.einsum("kb,ebc->ekc", mat_real, real_part, precision=HIGHEST) - jnp.einsum(
        "kb,ebc->ekc", mat_imag, imag_part, precision=HIGHEST
    )
    out_imag = jnp.einsum("kb,ebc->ekc", mat_real, imag_part, precision=HIGHEST) + jnp.einsum(
        "kb,ebc->ekc", mat_imag, real_part, precision=HIGHEST
    )
    return (out_real, out_imag)


def rotate_rows(real_part, imag_part, frequency_row, sign_value, total_rows):
    products = jnp.arange(real_part.shape[1], dtype=jnp.int32) * frequency_row
    phases = sign_value * 2.0 * math.pi / total_rows * products.astype(jnp.float32)
    cosine = jnp.cos(phases)[None, :, None]
    sine_value = jnp.sin(phases)[None, :, None]
    return (
        real_part * cosine - imag_part * sine_value,
        real_part * sine_value + imag_part * cosine,
    )


def pairs_forward(real_part, imag_part, device_index, bit_total):
    for section_bit in reversed(range(bit_total)):
        other_real, other_imag = swapped((real_part, imag_part), "ctx", section_bit)
        higher = device_index >> section_bit & 1 == 1
        within = (device_index % (1 << section_bit)).astype(jnp.float32)
        phase_angle = -2.0 * math.pi * within / float(2 << section_bit)
        cosine = jnp.cos(phase_angle)
        sine_value = jnp.sin(phase_angle)
        diff_real = other_real - real_part
        diff_imag = other_imag - imag_part
        turned_real = diff_real * cosine - diff_imag * sine_value
        turned_imag = diff_real * sine_value + diff_imag * cosine
        real_part = jnp.where(higher, turned_real, real_part + other_real)
        imag_part = jnp.where(higher, turned_imag, imag_part + other_imag)
    return (real_part, imag_part)


def pairs_inverse(real_part, imag_part, device_index, bit_total):
    for section_bit in range(bit_total):
        higher = device_index >> section_bit & 1 == 1
        within = (device_index % (1 << section_bit)).astype(jnp.float32)
        phase_angle = 2.0 * math.pi * within / float(2 << section_bit)
        cosine = jnp.cos(phase_angle)
        sine_value = jnp.sin(phase_angle)
        ready_real = jnp.where(higher, real_part * cosine - imag_part * sine_value, real_part)
        ready_imag = jnp.where(higher, real_part * sine_value + imag_part * cosine, imag_part)
        other_real, other_imag = swapped((ready_real, ready_imag), "ctx", section_bit)
        real_part = jnp.where(higher, other_real - ready_real, ready_real + other_real)
        imag_part = jnp.where(higher, other_imag - ready_imag, ready_imag + other_imag)
    return (real_part, imag_part)


def forward_spectrum(local_rows, device_index, frequency_row, total_rows):
    row_count = local_rows.shape[0]
    bit_total = lax.axis_size("ctx").bit_length() - 1
    positions = (device_index * row_count + jnp.arange(row_count, dtype=jnp.int32)).astype(
        jnp.float32
    )[:, None]
    phases = -math.pi / total_rows * positions
    real_part = jnp.stack([local_rows, local_rows * jnp.cos(phases)])
    imag_part = jnp.stack([jnp.zeros_like(local_rows), local_rows * jnp.sin(phases)])
    real_part, imag_part = pairs_forward(real_part, imag_part, device_index, bit_total)
    real_part, imag_part = rotate_rows(real_part, imag_part, frequency_row, -1.0, total_rows)
    return across_rows(real_part, imag_part, -1.0)


def inverse_rows(real_part, imag_part, device_index, frequency_row, total_rows):
    row_count = real_part.shape[1]
    bit_total = lax.axis_size("ctx").bit_length() - 1
    real_part, imag_part = across_rows(real_part, imag_part, 1.0)
    real_part, imag_part = rotate_rows(real_part, imag_part, frequency_row, 1.0, total_rows)
    real_part, imag_part = pairs_inverse(real_part, imag_part, device_index, bit_total)
    positions = (device_index * row_count + jnp.arange(row_count, dtype=jnp.int32)).astype(
        jnp.float32
    )[:, None]
    phases = math.pi / total_rows * positions
    combined = real_part[0] + real_part[1] * jnp.cos(phases) - imag_part[1] * jnp.sin(phases)
    return combined / (2.0 * total_rows)


def closed_spectrum(residue, decay_rate, frequencies, total_rows):
    angle = math.pi / total_rows * frequencies.astype(jnp.float32)
    cos_angle = jnp.cos(angle)[:, :, None]
    sin_angle = jnp.sin(angle)[:, :, None]
    versine = (2.0 * jnp.sin(0.5 * angle) ** 2)[:, :, None]
    parity = (1 - 2 * (frequencies % 2)).astype(jnp.float32)[:, :, None]
    shape_out = (frequencies.shape[0], frequencies.shape[1], residue.shape[1])
    spec_real = jnp.zeros(shape_out, jnp.float32)
    spec_imag = jnp.zeros(shape_out, jnp.float32)
    for order_mode in range(residue.shape[0]):
        rate = decay_rate[order_mode]
        amplitude = residue[order_mode] * jnp.sqrt(2.0 * rate)
        lost = -jnp.expm1(-rate)
        retained = jnp.exp(-rate)
        tail = jnp.exp(-rate * total_rows)
        numerator = amplitude * (1.0 - tail * parity)
        den_real = versine + cos_angle * lost
        den_imag = retained * sin_angle
        scale_value = numerator / (den_real * den_real + den_imag * den_imag)
        spec_real = spec_real + scale_value * den_real
        spec_imag = spec_imag - scale_value * den_imag
    return (spec_real, spec_imag)


def body(
    query_input, key_input, value_input, short_weight, residue, decay_rate, skip_gain, out_weight
):
    device_index = lax.axis_index("ctx")
    device_count = lax.axis_size("ctx")
    row_count = query_input.shape[0]
    total_rows = row_count * device_count
    tap_count = short_weight.shape[1]
    cut_row = row_count - tap_count + 1
    prior = passed_along(
        (query_input[cut_row:], key_input[cut_row:], value_input[cut_row:]), "ctx", 1
    )
    query_conv = short_filter(query_input, prior[0], short_weight[0])
    key_conv = short_filter(key_input, prior[1], short_weight[1])
    value_conv = short_filter(value_input, prior[2], short_weight[2])
    mixed_input = key_conv * value_conv
    bit_total = device_count.bit_length() - 1
    frequency_row = reversed_index(device_index, bit_total)
    signal_real, signal_imag = forward_spectrum(
        mixed_input, device_index, frequency_row, total_rows
    )
    frequencies = (
        2 * (frequency_row + device_count * jnp.arange(row_count, dtype=jnp.int32))[None, :]
        + jnp.arange(2, dtype=jnp.int32)[:, None]
    )
    filter_real, filter_imag = closed_spectrum(residue, decay_rate, frequencies, total_rows)
    product_real = signal_real * filter_real - signal_imag * filter_imag
    product_imag = signal_real * filter_imag + signal_imag * filter_real
    convolved = inverse_rows(product_real, product_imag, device_index, frequency_row, total_rows)
    gated = (query_conv * (convolved + skip_gain * mixed_input)).astype(jnp.bfloat16)
    partial_value = jnp.dot(gated, out_weight, preferred_element_type=jnp.float32)
    return lax.psum_scatter(
        partial_value.astype(jnp.bfloat16), "ch", scatter_dimension=1, tiled=True
    )


def solution(mesh):
    return jax.shard_map(
        body,
        mesh=mesh,
        in_specs=(
            P("ctx", "ch"),
            P("ctx", "ch"),
            P("ctx", "ch"),
            P(None, None, "ch"),
            P(None, "ch"),
            P(None, "ch"),
            P("ch"),
            P("ch", None),
        ),
        out_specs=P("ctx", "ch"),
        check_vma=False,
    )
```

profile of v0, /device:TPU:2, one launch (start us, length us, event | category | flops | bytes accessed | tf_op | source)
XLA Modules:
  0.0 415.9 jit_solution(10061828376152411717)
XLA Ops:
  7.4 3.4 collective-permute-start.1
  11.7 3.1 collective-permute-start.2
  14.9 0.9 fusion.108
  15.8 1.0 copy.16
  16.8 1.0 copy.18
  18.7 0.7 multiply_bitcast_fusion.1
  19.5 7.3 %collective-permute-start.3 = (f32[2,128,512]{1,2,0:T(8,128)S(1)}, f32[2,128,512]{1,2,0:T(8,128)S(1)}, u32[]{:S(2)}, u32[]{:S(2)}) collective-permute-start(f32[2,128,512]{1,2,0:T(8,128)S(1)} %pad_maximum_fusion), channel_id=1, source_target_pairs={{0,128},{8,136},{16,144},{24,152},{32,160},{40,168},{48,176},{56,1... | collective-permute-start | bytes 1572872 | tf_op jit(solution)/shard_map/ppermute | solution.py:15
  27.2 15.9 %collective-permute-done.3 = f32[2,128,512]{1,2,0:T(8,128)S(1)} collective-permute-done((f32[2,128,512]{1,2,0:T(8,128)S(1)}, f32[2,128,512]{1,2,0:T(8,128)S(1)}, u32[]{:S(2)}, u32[]{:S(2)}) %collective-permute-start.3) | collective-permute-done | bytes 524320 | tf_op jit(solution)/shard_map/ppermute | solution.py:15
  43.1 27.1 %collective-permute-done.4 = f32[2,128,512]{1,2,0:T(8,128)S(1)} collective-permute-done((f32[2,128,512]{1,2,0:T(8,128)S(1)}, f32[2,128,512]{1,2,0:T(8,128)S(1)}, u32[]{:S(2)}, u32[]{:S(2)}) %collective-permute-start.4) | collective-permute-done | bytes 524320 | tf_op jit(solution)/shard_map/ppermute | solution.py:15
  70.3 3.3 collective-permute-start.5
  73.9 33.7 %collective-permute-done.5 = f32[2,128,512]{1,2,0:T(8,128)S(1)} collective-permute-done((f32[2,128,512]{1,2,0:T(8,128)S(1)}, f32[2,128,512]{1,2,0:T(8,128)S(1)}, u32[]{:S(2)}, u32[]{:S(2)}) %collective-permute-start.5) | collective-permute-done | bytes 524320 | tf_op jit(solution)/shard_map/ppermute | solution.py:15
  107.6 11.0 %collective-permute-done.6 = f32[2,128,512]{1,2,0:T(8,128)S(1)} collective-permute-done((f32[2,128,512]{1,2,0:T(8,128)S(1)}, f32[2,128,512]{1,2,0:T(8,128)S(1)}, u32[]{:S(2)}, u32[]{:S(2)}) %collective-permute-start.6) | collective-permute-done | bytes 524320 | tf_op jit(solution)/shard_map/ppermute | solution.py:15
  118.9 2.0 collective-permute-start.8
  121.3 0.9 multiply_exponential_fusion.3
  122.2 11.5 %collective-permute-done.7 = f32[2,128,512]{1,2,0:T(8,128)S(1)} collective-permute-done((f32[2,128,512]{1,2,0:T(8,128)S(1)}, f32[2,128,512]{1,2,0:T(8,128)S(1)}, u32[]{:S(2)}, u32[]{:S(2)}) %collective-permute-start.7) | collective-permute-done | bytes 524320 | tf_op jit(solution)/shard_map/ppermute | solution.py:15
  133.7 10.1 %collective-permute-done.8 = f32[2,128,512]{1,2,0:T(8,128)S(1)} collective-permute-done((f32[2,128,512]{1,2,0:T(8,128)S(1)}, f32[2,128,512]{1,2,0:T(8,128)S(1)}, u32[]{:S(2)}, u32[]{:S(2)}) %collective-permute-start.8) | collective-permute-done | bytes 524320 | tf_op jit(solution)/shard_map/ppermute | solution.py:15
  144.0 2.6 collective-permute-start.10
  146.7 1.0 collective-permute-start.9
  147.7 1.1 sqrt_multiply_fusion.15
  148.8 1.1 multiply_exponential_fusion.15
  149.9 10.6 %collective-permute-done.10 = f32[2,128,512]{1,2,0:T(8,128)S(1)} collective-permute-done((f32[2,128,512]{1,2,0:T(8,128)S(1)}, f32[2,128,512]{1,2,0:T(8,128)S(1)}, u32[]{:S(2)}, u32[]{:S(2)}) %collective-permute-start.10) | collective-permute-done | bytes 524320 | tf_op jit(solution)/shard_map/ppermute | solution.py:15
  160.4 9.3 %collective-permute-done.9 = f32[2,128,512]{1,2,0:T(8,128)S(1)} collective-permute-done((f32[2,128,512]{1,2,0:T(8,128)S(1)}, f32[2,128,512]{1,2,0:T(8,128)S(1)}, u32[]{:S(2)}, u32[]{:S(2)}) %collective-permute-start.9) | collective-permute-done | bytes 524320 | tf_op jit(solution)/shard_map/ppermute | solution.py:15
  170.0 2.0 collective-permute-start.12
  172.1 1.0 exponential-minus-one_negate_fusion.15
  173.1 1.1 sqrt_multiply_fusion.14
  174.2 10.6 %collective-permute-done.11 = f32[2,128,512]{1,2,0:T(8,128)S(1)} collective-permute-done((f32[2,128,512]{1,2,0:T(8,128)S(1)}, f32[2,128,512]{1,2,0:T(8,128)S(1)}, u32[]{:S(2)}, u32[]{:S(2)}) %collective-permute-start.11) | collective-permute-done | bytes 524320 | tf_op jit(solution)/shard_map/ppermute | solution.py:15
  184.8 8.4 %collective-permute-done.12 = f32[2,128,512]{1,2,0:T(8,128)S(1)} collective-permute-done((f32[2,128,512]{1,2,0:T(8,128)S(1)}, f32[2,128,512]{1,2,0:T(8,128)S(1)}, u32[]{:S(2)}, u32[]{:S(2)}) %collective-permute-start.12) | collective-permute-done | bytes 524320 | tf_op jit(solution)/shard_map/ppermute | solution.py:15
  195.2 4.8 %multiply_subtract_fusion.1 = (f32[2,128,512]{1,2,0:T(8,128)S(1)}, f32[2,128,512]{1,2,0:T(8,128)S(1)}, f32[2,128,512]{1,2,0:T(8,128)S(1)}, f32[2,128,512]{1,2,0:T(8,128)S(1)}) fusion(f32[2,128,512]{1,2,0:T(8,128)S(1)} %fusion.1, f32[512]{0:T(512)S(1)} %bitcast.147, f32[512]{0:T(512)S(1)} %bitcast.209, f32[512]{0:T(512)S(1)} %bitcast.180, ...), kind=kOutput, calls=%fused_computation.112 | convolution fusion | flops 231473152 | bytes 4396032 | tf_op jit(solution)/shard_map/kb,ebc->ekc/dot_general | solution.py:55
  203.0 1.7 collective-permute-start.14
  204.9 12.6 %collective-permute-done.13 = f32[2,128,512]{1,2,0:T(8,128)S(1)} collective-permute-done((f32[2,128,512]{1,2,0:T(8,128)S(1)}, f32[2,128,512]{1,2,0:T(8,128)S(1)}, u32[]{:S(2)}, u32[]{:S(2)}) %collective-permute-start.13) | collective-permute-done | bytes 524320 | tf_op jit(solution)/shard_map/ppermute | solution.py:15
  217.5 8.8 %collective-permute-done.14 = f32[2,128,512]{1,2,0:T(8,128)S(1)} collective-permute-done((f32[2,128,512]{1,2,0:T(8,128)S(1)}, f32[2,128,512]{1,2,0:T(8,128)S(1)}, u32[]{:S(2)}, u32[]{:S(2)}) %collective-permute-start.14) | collective-permute-done | bytes 524320 | tf_op jit(solution)/shard_map/ppermute | solution.py:15
  226.7 3.5 collective-permute-start.16
  230.4 12.4 %collective-permute-done.15 = f32[2,128,512]{1,2,0:T(8,128)S(1)} collective-permute-done((f32[2,128,512]{1,2,0:T(8,128)S(1)}, f32[2,128,512]{1,2,0:T(8,128)S(1)}, u32[]{:S(2)}, u32[]{:S(2)}) %collective-permute-start.15) | collective-permute-done | bytes 524320 | tf_op jit(solution)/shard_map/ppermute | solution.py:15
  242.8 5.6 %collective-permute-done.16 = f32[2,128,512]{1,2,0:T(8,128)S(1)} collective-permute-done((f32[2,128,512]{1,2,0:T(8,128)S(1)}, f32[2,128,512]{1,2,0:T(8,128)S(1)}, u32[]{:S(2)}, u32[]{:S(2)}) %collective-permute-start.16) | collective-permute-done | bytes 524320 | tf_op jit(solution)/shard_map/ppermute | solution.py:15
  248.7 2.3 collective-permute-start.17
  251.3 12.5 %collective-permute-done.17 = f32[2,128,512]{1,2,0:T(8,128)S(1)} collective-permute-done((f32[2,128,512]{1,2,0:T(8,128)S(1)}, f32[2,128,512]{1,2,0:T(8,128)S(1)}, u32[]{:S(2)}, u32[]{:S(2)}) %collective-permute-start.17) | collective-permute-done | bytes 524320 | tf_op jit(solution)/shard_map/ppermute | solution.py:15
  263.8 6.6 %collective-permute-done.18 = f32[2,128,512]{1,2,0:T(8,128)S(1)} collective-permute-done((f32[2,128,512]{1,2,0:T(8,128)S(1)}, f32[2,128,512]{1,2,0:T(8,128)S(1)}, u32[]{:S(2)}, u32[]{:S(2)}) %collective-permute-start.18) | collective-permute-done | bytes 524320 | tf_op jit(solution)/shard_map/ppermute | solution.py:15
  270.6 8.2 %collective-permute-start.19 = (f32[2,128,512]{1,2,0:T(8,128)S(1)}, f32[2,128,512]{1,2,0:T(8,128)S(1)}, u32[]{:S(2)}, u32[]{:S(2)}) collective-permute-start(f32[2,128,512]{1,2,0:T(8,128)S(1)} %get-tuple-element.13), channel_id=1, source_target_pairs={{0,64},{8,72},{16,80},{24,88},{32,96},{40,104},{48,112},{56,120},{... | collective-permute-start | bytes 1572872 | tf_op jit(solution)/shard_map/ppermute | solution.py:15
  279.1 29.3 %collective-permute-done.19 = f32[2,128,512]{1,2,0:T(8,128)S(1)} collective-permute-done((f32[2,128,512]{1,2,0:T(8,128)S(1)}, f32[2,128,512]{1,2,0:T(8,128)S(1)}, u32[]{:S(2)}, u32[]{:S(2)}) %collective-permute-start.19) | collective-permute-done | bytes 524320 | tf_op jit(solution)/shard_map/ppermute | solution.py:15
  308.4 8.1 %collective-permute-done.20 = f32[2,128,512]{1,2,0:T(8,128)S(1)} collective-permute-done((f32[2,128,512]{1,2,0:T(8,128)S(1)}, f32[2,128,512]{1,2,0:T(8,128)S(1)}, u32[]{:S(2)}, u32[]{:S(2)}) %collective-permute-start.20) | collective-permute-done | bytes 524320 | tf_op jit(solution)/shard_map/ppermute | solution.py:15
  316.7 2.9 collective-permute-start.21
  319.6 3.1 collective-permute-start.22
  322.9 2.8 collective-permute-start
  325.9 4.2 %collective-permute-done = bf16[2,512]{0,1:T(8,128)(2,1)S(1)} collective-permute-done((bf16[2,512]{0,1:T(8,128)(2,1)S(1)}, bf16[2,512]{0,1:T(8,128)(2,1)S(1)}, u32[]{:S(2)}, u32[]{:S(2)}) %collective-permute-start) | collective-permute-done | bytes 2080 | tf_op jit(solution)/shard_map/ppermute | solution.py:21
  330.3 24.2 %collective-permute-done.21 = f32[2,128,512]{1,2,0:T(8,128)S(1)} collective-permute-done((f32[2,128,512]{1,2,0:T(8,128)S(1)}, f32[2,128,512]{1,2,0:T(8,128)S(1)}, u32[]{:S(2)}, u32[]{:S(2)}) %collective-permute-start.21) | collective-permute-done | bytes 524320 | tf_op jit(solution)/shard_map/ppermute | solution.py:15
  354.6 10.5 %collective-permute-done.22 = f32[2,128,512]{1,2,0:T(8,128)S(1)} collective-permute-done((f32[2,128,512]{1,2,0:T(8,128)S(1)}, f32[2,128,512]{1,2,0:T(8,128)S(1)}, u32[]{:S(2)}, u32[]{:S(2)}) %collective-permute-start.22) | collective-permute-done | bytes 524320 | tf_op jit(solution)/shard_map/ppermute | solution.py:15
  365.1 6.4 %convolution_convert_fusion = bf16[128,8192]{1,0:T(8,128)(2,1)} fusion(bf16[512,8192]{1,0:T(8,128)(2,1)} %param.19, f32[2,128,512]{1,2,0:T(8,128)S(1)} %add_select_fusion.2, f32[130,512]{0,1:T(8,128)S(1)} %maximum_convert_fusion, f32[128,512]{0,1:T(8,128)S(1)} %get-tuple-element.9, f32[2,128,512]{1,2,0:T(8,128)S(1)} %get-tuple-element.10, ...), kind=kOutput, calls=%fused_computation | convolution fusion | flops 1075904512 | bytes 12592129 | tf_op jit(solution)/shard_map/dot_general | solution.py:186
  371.5 37.5 %reduce-scatter.2.cloned.1.call-done = bf16[128,1024]{1,0:T(8,128)(2,1)} async-done(((bf16[128,8192]{1,0:T(8,128)(2,1)}), bf16[128,1024]{1,0:T(8,128)(2,1)}) %reduce-scatter.2.cloned.1.call-update) | async-done | bytes 262160 | tf_op jit(solution)/shard_map/reduce_scatter | solution.py:187
  (61 shorter events, 11.0 us)
Async XLA Ops:
  6.5 402.5 %reduce-scatter.2.cloned.1.call-start = ((), (), s32[]{:S(2)}) async-start(), calls=%async_computation.1 | async-start | bytes 2359296 | tf_op jit(solution)/shard_map/reduce_scatter | solution.py:187
  7.4 10.5 %collective-permute-start.1 = (bf16[2,512]{0,1:T(8,128)(2,1)S(1)}, bf16[2,512]{0,1:T(8,128)(2,1)S(1)}, u32[]{:S(2)}, u32[]{:S(2)}) collective-permute-start(bf16[2,512]{0,1:T(8,128)(2,1)S(1)} %copy.15), channel_id=1, source_target_pairs={{0,8},{8,16},{16,24},{24,32},{32,40},{40,48},{48,56},{56,64},{64,7... | collective-permute-start | bytes 6152 | tf_op jit(solution)/shard_map/ppermute | solution.py:21
  11.7 6.9 %collective-permute-start.2 = (bf16[2,512]{0,1:T(8,128)(2,1)S(1)}, bf16[2,512]{0,1:T(8,128)(2,1)S(1)}, u32[]{:S(2)}, u32[]{:S(2)}) collective-permute-start(bf16[2,512]{0,1:T(8,128)(2,1)S(1)} %copy.17), channel_id=1, source_target_pairs={{0,8},{8,16},{16,24},{24,32},{32,40},{40,48},{48,56},{56,64},{64,7... | collective-permute-start | bytes 6152 | tf_op jit(solution)/shard_map/ppermute | solution.py:21
  19.5 23.5 %collective-permute-start.3 = (f32[2,128,512]{1,2,0:T(8,128)S(1)}, f32[2,128,512]{1,2,0:T(8,128)S(1)}, u32[]{:S(2)}, u32[]{:S(2)}) collective-permute-start(f32[2,128,512]{1,2,0:T(8,128)S(1)} %pad_maximum_fusion), channel_id=1, source_target_pairs={{0,128},{8,136},{16,144},{24,152},{32,160},{40,168},{48,176},{56,1... | collective-permute-start | bytes 1572872 | tf_op jit(solution)/shard_map/ppermute | solution.py:15
  26.8 166.5 %copy-start.2 = (f32[128,128,1]{1,0,2:T(8,128)S(1)}, f32[128,128,1]{1,0,2:T(8,128)}, u32[]{:S(2)}) copy-start(f32[128,128,1]{1,0,2:T(8,128)} %constant.165) | copy-start | bytes 196612
  26.9 43.2 %collective-permute-start.4 = (f32[2,128,512]{1,2,0:T(8,128)S(1)}, f32[2,128,512]{1,2,0:T(8,128)S(1)}, u32[]{:S(2)}, u32[]{:S(2)}) collective-permute-start(f32[2,128,512]{1,2,0:T(8,128)S(1)} %stack.19), channel_id=1, source_target_pairs={{0,128},{8,136},{16,144},{24,152},{32,160},{40,168},{48,176},{56,1... | collective-permute-start | bytes 1572872 | tf_op jit(solution)/shard_map/ppermute | solution.py:15
  70.3 124.3 %copy-start = (f32[128,128,1]{1,0,2:T(8,128)S(1)}, f32[128,128,1]{1,0,2:T(8,128)}, u32[]{:S(2)}) copy-start(f32[128,128,1]{1,0,2:T(8,128)} %constant.164) | copy-start | bytes 196612
  70.3 37.3 %collective-permute-start.5 = (f32[2,128,512]{1,2,0:T(8,128)S(1)}, f32[2,128,512]{1,2,0:T(8,128)S(1)}, u32[]{:S(2)}, u32[]{:S(2)}) collective-permute-start(f32[2,128,512]{1,2,0:T(8,128)S(1)} %get-tuple-element.26), channel_id=1, source_target_pairs={{0,64},{8,72},{16,80},{24,88},{32,96},{40,104},{48,112},{56,120},{... | collective-permute-start | bytes 1572872 | tf_op jit(solution)/shard_map/ppermute | solution.py:15
  73.6 45.0 %collective-permute-start.6 = (f32[2,128,512]{1,2,0:T(8,128)S(1)}, f32[2,128,512]{1,2,0:T(8,128)S(1)}, u32[]{:S(2)}, u32[]{:S(2)}) collective-permute-start(f32[2,128,512]{1,2,0:T(8,128)S(1)} %get-tuple-element.27), channel_id=1, source_target_pairs={{0,64},{8,72},{16,80},{24,88},{32,96},{40,104},{48,112},{56,120},{... | collective-permute-start | bytes 1572872 | tf_op jit(solution)/shard_map/ppermute | solution.py:15
  118.8 14.9 %collective-permute-start.7 = (f32[2,128,512]{1,2,0:T(8,128)S(1)}, f32[2,128,512]{1,2,0:T(8,128)S(1)}, u32[]{:S(2)}, u32[]{:S(2)}) collective-permute-start(f32[2,128,512]{1,2,0:T(8,128)S(1)} %get-tuple-element.24), channel_id=1, source_target_pairs={{0,32},{8,40},{16,48},{24,56},{32,0},{40,8},{48,16},{56,24},{64,96... | collective-permute-start | bytes 1572872 | tf_op jit(solution)/shard_map/ppermute | solution.py:15
  118.9 24.9 %collective-permute-start.8 = (f32[2,128,512]{1,2,0:T(8,128)S(1)}, f32[2,128,512]{1,2,0:T(8,128)S(1)}, u32[]{:S(2)}, u32[]{:S(2)}) collective-permute-start(f32[2,128,512]{1,2,0:T(8,128)S(1)} %get-tuple-element.25), channel_id=1, source_target_pairs={{0,32},{8,40},{16,48},{24,56},{32,0},{40,8},{48,16},{56,24},{64,96... | collective-permute-start | bytes 1572872 | tf_op jit(solution)/shard_map/ppermute | solution.py:15
  144.0 16.4 %collective-permute-start.10 = (f32[2,128,512]{1,2,0:T(8,128)S(1)}, f32[2,128,512]{1,2,0:T(8,128)S(1)}, u32[]{:S(2)}, u32[]{:S(2)}) collective-permute-start(f32[2,128,512]{1,2,0:T(8,128)S(1)} %get-tuple-element.23), channel_id=1, source_target_pairs={{0,16},{8,24},{16,0},{24,8},{32,48},{40,56},{48,32},{56,40},{64,80... | collective-permute-start | bytes 1572872 | tf_op jit(solution)/shard_map/ppermute | solution.py:15
  146.7 23.0 %collective-permute-start.9 = (f32[2,128,512]{1,2,0:T(8,128)S(1)}, f32[2,128,512]{1,2,0:T(8,128)S(1)}, u32[]{:S(2)}, u32[]{:S(2)}) collective-permute-start(f32[2,128,512]{1,2,0:T(8,128)S(1)} %get-tuple-element.22), channel_id=1, source_target_pairs={{0,16},{8,24},{16,0},{24,8},{32,48},{40,56},{48,32},{56,40},{64,80... | collective-permute-start | bytes 1572872 | tf_op jit(solution)/shard_map/ppermute | solution.py:15
  169.9 14.9 %collective-permute-start.11 = (f32[2,128,512]{1,2,0:T(8,128)S(1)}, f32[2,128,512]{1,2,0:T(8,128)S(1)}, u32[]{:S(2)}, u32[]{:S(2)}) collective-permute-start(f32[2,128,512]{1,2,0:T(8,128)S(1)} %get-tuple-element.20), channel_id=1, source_target_pairs={{0,8},{8,0},{16,24},{24,16},{32,40},{40,32},{48,56},{56,48},{64,72... | collective-permute-start | bytes 1572872 | tf_op jit(solution)/shard_map/ppermute | solution.py:15
  170.0 23.2 %collective-permute-start.12 = (f32[2,128,512]{1,2,0:T(8,128)S(1)}, f32[2,128,512]{1,2,0:T(8,128)S(1)}, u32[]{:S(2)}, u32[]{:S(2)}) collective-permute-start(f32[2,128,512]{1,2,0:T(8,128)S(1)} %get-tuple-element.21), channel_id=1, source_target_pairs={{0,8},{8,0},{16,24},{24,16},{32,40},{40,32},{48,56},{56,48},{64,72... | collective-permute-start | bytes 1572872 | tf_op jit(solution)/shard_map/ppermute | solution.py:15
  195.2 6.1 %copy-start.1 = (f32[128,128,1]{1,0,2:T(8,128)S(1)}, f32[128,128,1]{1,0,2:T(8,128)}, u32[]{:S(2)}) copy-start(f32[128,128,1]{1,0,2:T(8,128)} %constant.166) | copy-start | bytes 196612
  201.3 121.4 %copy-start.3 = (bf16[128,512]{1,0:T(8,128)(2,1)S(1)}, bf16[128,512]{1,0:T(8,128)(2,1)}, u32[]{:S(2)}) copy-start(bf16[128,512]{1,0:T(8,128)(2,1)} %param.12) | copy-start | bytes 393220
  201.9 163.2 %copy-start.4 = (f32[512]{0:T(512)S(1)}, f32[512]{0:T(512)}, u32[]{:S(2)}) copy-start(f32[512]{0:T(512)} %param.18) | copy-start | bytes 6148
  202.7 14.9 %collective-permute-start.13 = (f32[2,128,512]{1,2,0:T(8,128)S(1)}, f32[2,128,512]{1,2,0:T(8,128)S(1)}, u32[]{:S(2)}, u32[]{:S(2)}) collective-permute-start(f32[2,128,512]{1,2,0:T(8,128)S(1)} %get-tuple-element.29), channel_id=1, source_target_pairs={{0,8},{8,0},{16,24},{24,16},{32,40},{40,32},{48,56},{56,48},{64,72... | collective-permute-start | bytes 1572872 | tf_op jit(solution)/shard_map/ppermute | solution.py:15
  203.0 23.4 %collective-permute-start.14 = (f32[2,128,512]{1,2,0:T(8,128)S(1)}, f32[2,128,512]{1,2,0:T(8,128)S(1)}, u32[]{:S(2)}, u32[]{:S(2)}) collective-permute-start(f32[2,128,512]{1,2,0:T(8,128)S(1)} %get-tuple-element.28), channel_id=1, source_target_pairs={{0,8},{8,0},{16,24},{24,16},{32,40},{40,32},{48,56},{56,48},{64,72... | collective-permute-start | bytes 1572872 | tf_op jit(solution)/shard_map/ppermute | solution.py:15
  226.6 16.2 %collective-permute-start.15 = (f32[2,128,512]{1,2,0:T(8,128)S(1)}, f32[2,128,512]{1,2,0:T(8,128)S(1)}, u32[]{:S(2)}, u32[]{:S(2)}) collective-permute-start(f32[2,128,512]{1,2,0:T(8,128)S(1)} %get-tuple-element.17), channel_id=1, source_target_pairs={{0,16},{8,24},{16,0},{24,8},{32,48},{40,56},{48,32},{56,40},{64,80... | collective-permute-start | bytes 1572872 | tf_op jit(solution)/shard_map/ppermute | solution.py:15
  226.7 21.7 %collective-permute-start.16 = (f32[2,128,512]{1,2,0:T(8,128)S(1)}, f32[2,128,512]{1,2,0:T(8,128)S(1)}, u32[]{:S(2)}, u32[]{:S(2)}) collective-permute-start(f32[2,128,512]{1,2,0:T(8,128)S(1)} %get-tuple-element.16), channel_id=1, source_target_pairs={{0,16},{8,24},{16,0},{24,8},{32,48},{40,56},{48,32},{56,40},{64,80... | collective-permute-start | bytes 1572872 | tf_op jit(solution)/shard_map/ppermute | solution.py:15
  248.7 15.1 %collective-permute-start.17 = (f32[2,128,512]{1,2,0:T(8,128)S(1)}, f32[2,128,512]{1,2,0:T(8,128)S(1)}, u32[]{:S(2)}, u32[]{:S(2)}) collective-permute-start(f32[2,128,512]{1,2,0:T(8,128)S(1)} %get-tuple-element.15), channel_id=1, source_target_pairs={{0,32},{8,40},{16,48},{24,56},{32,0},{40,8},{48,16},{56,24},{64,96... | collective-permute-start | bytes 1572872 | tf_op jit(solution)/shard_map/ppermute | solution.py:15
  251.0 19.3 %collective-permute-start.18 = (f32[2,128,512]{1,2,0:T(8,128)S(1)}, f32[2,128,512]{1,2,0:T(8,128)S(1)}, u32[]{:S(2)}, u32[]{:S(2)}) collective-permute-start(f32[2,128,512]{1,2,0:T(8,128)S(1)} %get-tuple-element.14), channel_id=1, source_target_pairs={{0,32},{8,40},{16,48},{24,56},{32,0},{40,8},{48,16},{56,24},{64,96... | collective-permute-start | bytes 1572872 | tf_op jit(solution)/shard_map/ppermute | solution.py:15
  270.6 37.8 %collective-permute-start.19 = (f32[2,128,512]{1,2,0:T(8,128)S(1)}, f32[2,128,512]{1,2,0:T(8,128)S(1)}, u32[]{:S(2)}, u32[]{:S(2)}) collective-permute-start(f32[2,128,512]{1,2,0:T(8,128)S(1)} %get-tuple-element.13), channel_id=1, source_target_pairs={{0,64},{8,72},{16,80},{24,88},{32,96},{40,104},{48,112},{56,120},{... | collective-permute-start | bytes 1572872 | tf_op jit(solution)/shard_map/ppermute | solution.py:15
  278.8 37.6 %collective-permute-start.20 = (f32[2,128,512]{1,2,0:T(8,128)S(1)}, f32[2,128,512]{1,2,0:T(8,128)S(1)}, u32[]{:S(2)}, u32[]{:S(2)}) collective-permute-start(f32[2,128,512]{1,2,0:T(8,128)S(1)} %get-tuple-element.12), channel_id=1, source_target_pairs={{0,64},{8,72},{16,80},{24,88},{32,96},{40,104},{48,112},{56,120},{... | collective-permute-start | bytes 1572872 | tf_op jit(solution)/shard_map/ppermute | solution.py:15
  316.7 37.8 %collective-permute-start.21 = (f32[2,128,512]{1,2,0:T(8,128)S(1)}, f32[2,128,512]{1,2,0:T(8,128)S(1)}, u32[]{:S(2)}, u32[]{:S(2)}) collective-permute-start(f32[2,128,512]{1,2,0:T(8,128)S(1)} %get-tuple-element.11), channel_id=1, source_target_pairs={{0,128},{8,136},{16,144},{24,152},{32,160},{40,168},{48,176},{56,1... | collective-permute-start | bytes 1572872 | tf_op jit(solution)/shard_map/ppermute | solution.py:15
  319.6 45.5 %collective-permute-start.22 = (f32[2,128,512]{1,2,0:T(8,128)S(1)}, f32[2,128,512]{1,2,0:T(8,128)S(1)}, u32[]{:S(2)}, u32[]{:S(2)}) collective-permute-start(f32[2,128,512]{1,2,0:T(8,128)S(1)} %get-tuple-element.10), channel_id=1, source_target_pairs={{0,128},{8,136},{16,144},{24,152},{32,160},{40,168},{48,176},{56,1... | collective-permute-start | bytes 1572872 | tf_op jit(solution)/shard_map/ppermute | solution.py:15
  322.9 7.2 %collective-permute-start = (bf16[2,512]{0,1:T(8,128)(2,1)S(1)}, bf16[2,512]{0,1:T(8,128)(2,1)S(1)}, u32[]{:S(2)}, u32[]{:S(2)}) collective-permute-start(bf16[2,512]{0,1:T(8,128)(2,1)S(1)} %copy.13), channel_id=1, source_target_pairs={{0,8},{8,16},{16,24},{24,32},{32,40},{40,48},{48,56},{56,64},{64,7... | collective-permute-start | bytes 6152 | tf_op jit(solution)/shard_map/ppermute | solution.py:21
Sparse Core Ops, SparseCore 0:
  371.6 37.3 reduce-scatter.1
where the time goes:
time: 417 us; the launch traced here: 416 us
  waiting for transfers between devices  321 us (77%)
  starting transfers between devices  50.4 us (12%)
  matrix products  15.4 us (4%)
  between operations  15.1 us (4%)
  other arithmetic  8.9 us (2%)
  local copies, waits for them, and re-layouts  5.08 us (1%)
    ppermute x20, waiting for transfers between devices, swapped(): return lax.ppermute(value, axis, pairs)  279 us
    ppermute x20, starting transfers between devices, swapped(): return lax.ppermute(value, axis, pairs)  41 us
    reduce_scatter x1, waiting for transfers between devices, body(): lax.psum_scatter(partial_value.astype(jnp.bfloat16), 'ch', scatter_dimens...  37.5 us
    ppermute x3, starting transfers between devices, passed_along(): return lax.ppermute(block, axis, route)  9.35 us
  transfers between devices with their start and end apart: 24, of which 23 were waited for; matrix products, arithmetic and copies ran while one was open for 2% of the time, Pallas kernels for 0%

commit v1 on v0

v1 whole, which is shorter than its diff:
```python
import functools

import jax
import jax.numpy as jnp
from jax import lax
from jax.experimental import pallas as pl
from jax.experimental.pallas import tpu as pltpu
from jax.sharding import PartitionSpec as P

F32 = jnp.float32
BF16 = jnp.bfloat16
ROWS = 8
LANES = 128
REDUCE = "a2a"
ZSTAGE = "perm"


def edge_kernel(q_ref, k_ref, v_ref, out_ref):
    out_ref[...] = jnp.concatenate([r[...].astype(F32) for r in (q_ref, k_ref, v_ref)], axis=0)


def edge_rows(q, k, v):
    rows, width = q.shape
    spec = pl.BlockSpec((16, width), lambda i: (rows // 16 - 1, 0))
    return pl.pallas_call(
        edge_kernel,
        grid=(1,),
        in_specs=[spec] * 3,
        out_specs=pl.BlockSpec((48, width), lambda i: (0, 0)),
        out_shape=jax.ShapeDtypeStruct((48, width), F32),
        name="edge",
    )(q, k, v)


def short_filter(x, earlier, taps):
    row = lax.broadcasted_iota(jnp.int32, x.shape, 0)
    one = jnp.where(row == 0, earlier[15:16], pltpu.roll(x, 1, 0))
    two = jnp.where(row == 0, earlier[14:15], jnp.where(row == 1, earlier[15:16], pltpu.roll(x, 2, 0)))
    return taps[0:1] * x + taps[1:2] * one + taps[2:3] * two


def state_kernel(q_ref, k_ref, v_ref, e_ref, w_ref, d_ref, query_ref, mixed_ref, state_ref):
    query_ref[...] = short_filter(q_ref[...].astype(F32), e_ref[0:16], w_ref[0])
    keys = short_filter(k_ref[...].astype(F32), e_ref[16:32], w_ref[1])
    values = short_filter(v_ref[...].astype(F32), e_ref[32:48], w_ref[2])
    mixed_ref[...] = keys * values
    rate = d_ref[...]
    order = rate.shape[0]
    fall = jnp.exp(-float(ROWS) * rate)
    falls = [jnp.broadcast_to(fall[r : r + 1], (ROWS, LANES)) for r in range(order)]
    sums = [jnp.zeros((ROWS, LANES), F32) for _ in range(order)]
    for i in range(mixed_ref.shape[0] // ROWS):
        tile = mixed_ref[i * ROWS : (i + 1) * ROWS]
        sums = [s * f + tile for s, f in zip(sums, falls)]
    left = (ROWS - 1 - lax.broadcasted_iota(jnp.int32, (ROWS, LANES), 0)).astype(F32)
    for r in range(order):
        weighed = sums[r] * jnp.exp(-rate[r : r + 1] * left)
        state_ref[r : r + 1] = jnp.sum(weighed, axis=0, keepdims=True)


def lane_spec(shape):
    lead = len(shape) - 1
    return pl.BlockSpec(tuple(shape[:-1]) + (LANES,), lambda i: (0,) * lead + (i,))


def lane_call(kernel, arrays, outs, name, scratch=(), flops=10**7):
    width = arrays[0].shape[-1]
    return pl.pallas_call(
        kernel,
        grid=(width // LANES,),
        in_specs=[lane_spec(a.shape) for a in arrays],
        out_specs=[lane_spec(o) for o in outs],
        out_shape=[jax.ShapeDtypeStruct(o, F32) for o in outs],
        scratch_shapes=list(scratch),
        cost_estimate=pl.CostEstimate(flops=flops, bytes_accessed=10**6, transcendentals=10**5),
        name=name,
    )(*arrays)


def local_kernel(mixed_ref, res_ref, d_ref, skip_ref, out_ref, impulse_ref):
    rate = d_ref[...]
    order = rate.shape[0]
    tiles = mixed_ref.shape[0] // ROWS
    size = res_ref[...] * jnp.sqrt(2.0 * rate)
    fall = jnp.exp(-float(ROWS) * rate)
    row = lax.broadcasted_iota(jnp.int32, (ROWS, LANES), 0).astype(F32)
    modes = [size[r : r + 1] * jnp.exp(-rate[r : r + 1] * row) for r in range(order)]
    falls = [jnp.broadcast_to(fall[r : r + 1], (ROWS, LANES)) for r in range(order)]
    for m in range(tiles):
        impulse_ref[m * ROWS : (m + 1) * ROWS] = sum(modes[1:], modes[0])
        modes = [a * f for a, f in zip(modes, falls)]
    skip = jnp.broadcast_to(skip_ref[...], (ROWS, LANES))
    mixed = mixed_ref[...]
    position = lax.broadcasted_iota(jnp.int32, mixed.shape, 0)
    for j in range(ROWS):
        moved = mixed if j == 0 else jnp.where(position < j, 0.0, pltpu.roll(mixed, j, 0))
        pieces = [moved[i * ROWS : (i + 1) * ROWS] for i in range(tiles)]
        if j == 0:
            sums = [skip * piece for piece in pieces]
        else:
            sums = [out_ref[i * ROWS : (i + 1) * ROWS] for i in range(tiles)]
        for m in range(tiles):
            weight = jnp.broadcast_to(impulse_ref[m * ROWS + j : m * ROWS + j + 1], (ROWS, LANES))
            for i in range(m, tiles):
                sums[i] = sums[i] + weight * pieces[i - m]
        for i in range(tiles):
            out_ref[i * ROWS : (i + 1) * ROWS] = sums[i]


def group_kernel(span, own_ref, r1_ref, r2_ref, r3_ref, d_ref, total_ref, before_ref):
    x = lax.axis_index("ctx") % 4
    rate = d_ref[...] * float(span)
    total = own_ref[...] * jnp.exp(-rate * (3 - x).astype(F32))
    before = jnp.zeros_like(total)
    for d, ref in ((1, r1_ref), (2, r2_ref), (3, r3_ref)):
        source = (x + 4 - d) % 4
        got = ref[...]
        total = total + got * jnp.exp(-rate * (3 - source).astype(F32))
        before = before + jnp.where(x >= d, got * jnp.exp(-rate * float(d - 1)), 0.0)
    total_ref[...] = total
    before_ref[...] = before


def gate_kernel(span, query_ref, local_ref, before_ref, res_ref, d_ref, *rest):
    *far, out_ref = rest
    x = (lax.axis_index("ctx") % 4).astype(F32)
    rate = d_ref[...]
    order = rate.shape[0]
    step = jnp.exp(-rate * float(4 * span))
    carried = far[-1][...]
    for ref in far[-2::-1]:
        carried = carried * step + ref[...]
    carry = before_ref[...] + carried * jnp.exp(-rate * (span * x))
    carry = carry * res_ref[...] * jnp.sqrt(2.0 * rate)
    fall = jnp.exp(-float(ROWS) * rate)
    row = lax.broadcasted_iota(jnp.int32, (ROWS, LANES), 0).astype(F32) + 1.0
    modes = [carry[r : r + 1] * jnp.exp(-rate[r : r + 1] * row) for r in range(order)]
    falls = [jnp.broadcast_to(fall[r : r + 1], (ROWS, LANES)) for r in range(order)]
    for i in range(span // ROWS):
        at = slice(i * ROWS, (i + 1) * ROWS)
        total = local_ref[at] + sum(modes[1:], modes[0])
        out_ref[at] = query_ref[at] * total
        modes = [a * f for a, f in zip(modes, falls)]


def project_kernel(gated_ref, w_ref, out_ref):
    out_ref[0] = jnp.dot(gated_ref[...].astype(BF16), w_ref[...], preferred_element_type=F32).astype(BF16)


def project(gated, weight, parts):
    rows, depth = gated.shape
    width = weight.shape[1] // parts
    return pl.pallas_call(
        project_kernel,
        grid=(parts,),
        in_specs=[
            pl.BlockSpec((rows, depth), lambda i: (0, 0)),
            pl.BlockSpec((depth, width), lambda i: (0, i)),
        ],
        out_specs=pl.BlockSpec((1, rows, width), lambda i: (i, 0, 0)),
        out_shape=jax.ShapeDtypeStruct((parts, rows, width), BF16),
        name="project",
    )(gated, weight)


def piece_kernel(at_ref, gated_ref, w_ref, out_ref):
    out_ref[...] = jnp.dot(gated_ref[...].astype(BF16), w_ref[...], preferred_element_type=F32).astype(BF16)


def piece(gated, weight, parts, at):
    rows, depth = gated.shape
    width = weight.shape[1] // parts
    return pl.pallas_call(
        piece_kernel,
        grid_spec=pltpu.PrefetchScalarGridSpec(
            num_scalar_prefetch=1,
            grid=(2,),
            in_specs=[
                pl.BlockSpec((rows, depth), lambda i, at: (0, 0)),
                pl.BlockSpec((depth, width // 2), lambda i, at: (0, 2 * at[0] + i)),
            ],
            out_specs=pl.BlockSpec((rows, width // 2), lambda i, at: (0, i)),
        ),
        out_shape=jax.ShapeDtypeStruct((rows, width), BF16),
        cost_estimate=pl.CostEstimate(flops=2 * rows * depth * width, bytes_accessed=2 * depth * width, transcendentals=0),
        name="piece",
    )(at, gated, weight)


def reduce_parts(gated, weight):
    parts = lax.axis_size("ch")
    if REDUCE == "perm":
        me = lax.axis_index("ch")
        got = []
        for d in (4, 3, 5, 2, 6, 7, 1):
            mine = piece(gated, weight, parts, ((me + d) % parts).astype(jnp.int32).reshape(1))
            pairs = [(i, (i + d) % parts) for i in range(parts)]
            got.append(lax.ppermute(mine, "ch", pairs))
        total = piece(gated, weight, parts, me.astype(jnp.int32).reshape(1)).astype(F32)
        for one in got:
            total = total + one.astype(F32)
        return total.astype(BF16)
    partial = project(gated, weight, parts)
    if REDUCE == "a2a":
        got = lax.all_to_all(partial, "ch", 0, 0, tiled=True)
        return jnp.sum(got.astype(F32), axis=0).astype(BF16)
    return lax.psum_scatter(partial, "ch", scatter_dimension=0, tiled=False)


def body(query_input, key_input, value_input, short_weight, residue, decay_rate, skip_gain, out_weight):
    count = lax.axis_size("ctx")
    rows, width = query_input.shape
    order = residue.shape[0]
    edge = edge_rows(query_input, key_input, value_input)
    edge = lax.ppermute(edge, "ctx", [(i, i + 1) for i in range(count - 1)])
    query, mixed, state = lane_call(
        state_kernel,
        [query_input, key_input, value_input, edge, short_weight, decay_rate],
        [(rows, width), (rows, width), (order, width)],
        "state",
    )
    near = []
    for d in (1, 2, 3):
        pairs = [(4 * z + x, 4 * z + (x + d) % 4) for z in range(count // 4) for x in range(4)]
        near.append(lax.ppermute(state, "ctx", pairs))
    (local,) = lane_call(
        local_kernel,
        [mixed, residue, decay_rate, skip_gain[None, :]],
        [(rows, width)],
        "local",
        scratch=[pltpu.VMEM((rows, LANES), F32)],
        flops=10**9,
    )
    total, before = lane_call(
        functools.partial(group_kernel, rows),
        [state, *near, decay_rate],
        [(order, width), (order, width)],
        "group",
    )
    far = []
    for d in range(1, count // 4):
        pairs = [(i, i + 4 * d) for i in range(count - 4 * d)]
        far.append(lax.ppermute(total, "ctx", pairs))
    (gated,) = lane_call(
        functools.partial(gate_kernel, rows),
        [query, local, before, residue, decay_rate, *far],
        [(rows, width)],
        "gate",
    )
    return reduce_parts(gated, out_weight)


def solution(mesh):
    return jax.shard_map(
        body,
        mesh=mesh,
        in_specs=(
            P("ctx", "ch"),
            P("ctx", "ch"),
            P("ctx", "ch"),
            P(None, None, "ch"),
            P(None, "ch"),
            P(None, "ch"),
            P("ch"),
            P("ch", None),
        ),
        out_specs=P("ctx", "ch"),
        check_vma=False,
    )
```

time: 417 us -> 96.1 us (0.23)
  waiting for transfers between devices: 321 us -> 5.65 us
  blocking collectives: 0 us -> 31.7 us
  Pallas kernels: 0 us -> 22.7 us
  starting transfers between devices: 50.4 us -> 31.1 us
  matrix products: 15.4 us -> 0 us
  between operations: 15.1 us -> 0.2 us
  other arithmetic: 8.9 us -> 1.1 us
    ppermute x23 -> x11, waiting for transfers between devices: 284 us -> 5.65 us  [the longest x1 3.31 us: body(): edge = lax.ppermute(edge, 'ctx', [(i, i + 1) for i in range(count - 1)])]
    reduce_scatter x1 -> x0, waiting for transfers between devices: 37.5 us -> none  [body(): lax.psum_scatter(partial_value.astype(jnp.bfloat16), 'ch', scatter_dimens...]
    all_to_all x0 -> x1, blocking collectives: none -> 31.7 us  [reduce_parts(): got = lax.all_to_all(partial, 'ch', 0, 0, tiled=True)]
    pallas_call x0 -> x6, Pallas kernels: none -> 22.7 us  [the longest x4 13.2 us: lane_call(): pl.pallas_call(kernel, grid=(width // LANES,), in_specs=[lane_spec(a.shap...]
    ppermute x23 -> x11, starting transfers between devices: 50.4 us -> 31.1 us  [the longest x7 23 us: body(): far.append(lax.ppermute(total, 'ctx', pairs))]
    dot_general x9 -> x0, matrix products: 15.4 us -> none  [the longest x1 6.39 us: body(): jnp.dot(gated, out_weight, preferred_element_type=jnp.float32)]
  transfers between devices with their start and end apart: 24 -> 11, of which waited for: 23 -> 3; matrix products, arithmetic and copies ran while one was open for 2% -> 0% of each run, Pallas kernels for 0% -> 4%
where the time goes in v1:
time: 96.1 us; the launch traced here: 94.3 us
  blocking collectives  31.7 us (33%)
  starting transfers between devices  31.1 us (32%)
  Pallas kernels  22.7 us (24%)
  waiting for transfers between devices  5.65 us (6%)
  local copies, waits for them, and re-layouts  1.83 us (2%)
  other arithmetic  1.1 us (1%)
    all_to_all x1, blocking collectives, reduce_parts(): got = lax.all_to_all(partial, 'ch', 0, 0, tiled=True)  31.7 us
    ppermute x7, starting transfers between devices, body(): far.append(lax.ppermute(total, 'ctx', pairs))  23 us
    pallas_call x4, Pallas kernels, lane_call(): pl.pallas_call(kernel, grid=(width // LANES,), in_specs=[lane_spec(a.shap...  13.2 us
    pallas_call x1, Pallas kernels, project(): pl.pallas_call(project_kernel, grid=(parts,), in_specs=[pl.BlockSpec((row...  8.1 us
    ppermute x3, starting transfers between devices, body(): near.append(lax.ppermute(state, 'ctx', pairs))  4.76 us
    ppermute x1, starting transfers between devices, body(): edge = lax.ppermute(edge, 'ctx', [(i, i + 1) for i in range(count - 1)])  3.39 us
    ppermute x1, waiting for transfers between devices, body(): edge = lax.ppermute(edge, 'ctx', [(i, i + 1) for i in range(count - 1)])  3.31 us
    ppermute x3, waiting for transfers between devices, body(): near.append(lax.ppermute(state, 'ctx', pairs))  2.32 us
  transfers between devices with their start and end apart: 11, of which 3 were waited for; matrix products, arithmetic and copies ran while one was open for 0% of the time, Pallas kernels for 4%

profile of v1, /device:TPU:2, one launch (start us, length us, event | category | flops | bytes accessed | tf_op | source)
XLA Modules:
  0.0 94.3 jit_solution(7018446990178164640)
XLA Ops:
  0.0 1.4 %edge.1 = f32[48,512]{1,0:T(8,128)} custom-call(bf16[128,512]{1,0:T(8,128)(2,1)} %q_ref.3, bf16[128,512]{1,0:T(8,128)(2,1)} %k_ref.3, bf16[128,512]{1,0:T(8,128)(2,1)} %v_ref.3), custom_call_target="tpu_custom_call" | custom-call | tf_op jit(solution)/shard_map/edge/pallas_call | solution.py:25
  1.4 3.4 %collective-permute-start = (f32[48,512]{1,0:T(8,128)}, f32[48,512]{1,0:T(8,128)S(1)}, u32[]{:S(2)}, u32[]{:S(2)}) collective-permute-start(f32[48,512]{1,0:T(8,128)} %edge.1), channel_id=1, source_target_pairs={{0,8},{8,16},{16,24},{24,32},{32,40},{40,48},{48,56},{56,64},{64,7... | collective-permute-start | bytes 294920 | tf_op jit(solution)/shard_map/ppermute | solution.py:215
  4.8 3.3 %collective-permute-done.e_ref = f32[48,512]{1,0:T(8,128)S(1)} collective-permute-done((f32[48,512]{1,0:T(8,128)}, f32[48,512]{1,0:T(8,128)S(1)}, u32[]{:S(2)}, u32[]{:S(2)}) %collective-permute-start) | collective-permute-done | bytes 98336 | tf_op jit(solution)/shard_map/ppermute | solution.py:215
  8.1 0.0 copy-start
  8.1 0.6 copy-done
  8.7 3.2 %state.1 = (f32[128,512]{1,0:T(8,128)}, f32[128,512]{1,0:T(8,128)}, f32[16,512]{1,0:T(8,128)}) custom-call(bf16[128,512]{1,0:T(8,128)(2,1)} %q_ref.3, bf16[128,512]{1,0:T(8,128)(2,1)} %k_ref.3, bf16[128,512]{1,0:T(8,128)(2,1)} %v_ref.3, f32[48,512]{1,0:T(8,128)} %copy-done, f32[3,3,512]{2,1,0:T(4,128)} %w_ref.2, f32[16,512]{1,0:T(8,128)} %d_ref.7), custom_call_target="tpu_custom_call" | custom-call | flops 10000000 | bytes 1000000 | tf_op jit(solution)/shard_map/state/pallas_call | solution.py:68
  11.9 0.0 collective-permute-start.3
  11.9 2.9 %collective-permute-start.2 = (f32[16,512]{1,0:T(8,128)}, f32[16,512]{1,0:T(8,128)S(1)}, u32[]{:S(2)}, u32[]{:S(2)}) collective-permute-start(f32[16,512]{1,0:T(8,128)} %get-tuple-element.12.own_ref), channel_id=1, source_target_pairs={{0,16},{8,24},{16,0},{24,8},{32,48},{40,56},{48,32},{56,40},{64,80... | collective-permute-start | bytes 98312 | tf_op jit(solution)/shard_map/ppermute | solution.py:225
  14.9 1.8 %collective-permute-start.1 = (f32[16,512]{1,0:T(8,128)}, f32[16,512]{1,0:T(8,128)S(1)}, u32[]{:S(2)}, u32[]{:S(2)}) collective-permute-start(f32[16,512]{1,0:T(8,128)} %get-tuple-element.12.own_ref), channel_id=1, source_target_pairs={{0,8},{8,16},{16,24},{24,0},{32,40},{40,48},{48,56},{56,32},{64,72... | collective-permute-start | bytes 98312 | tf_op jit(solution)/shard_map/ppermute | solution.py:225
  16.7 0.0 collective-permute-done.3.r3_ref
  16.7 1.0 %collective-permute-done.2.r2_ref = f32[16,512]{1,0:T(8,128)S(1)} collective-permute-done((f32[16,512]{1,0:T(8,128)}, f32[16,512]{1,0:T(8,128)S(1)}, u32[]{:S(2)}, u32[]{:S(2)}) %collective-permute-start.2) | collective-permute-done | bytes 32800 | tf_op jit(solution)/shard_map/ppermute | solution.py:225
  17.7 1.3 %collective-permute-done.1.r1_ref = f32[16,512]{1,0:T(8,128)S(1)} collective-permute-done((f32[16,512]{1,0:T(8,128)}, f32[16,512]{1,0:T(8,128)S(1)}, u32[]{:S(2)}, u32[]{:S(2)}) %collective-permute-start.1) | collective-permute-done | bytes 32800 | tf_op jit(solution)/shard_map/ppermute | solution.py:225
  19.0 0.0 copy-done.8
  19.0 0.0 copy-done.9
  19.0 0.6 copy-done.10
  19.6 2.8 %group.1 = (f32[16,512]{1,0:T(8,128)}, f32[16,512]{1,0:T(8,128)}) custom-call(f32[16,512]{1,0:T(8,128)} %get-tuple-element.12.own_ref, f32[16,512]{1,0:T(8,128)} %copy-done.10, f32[16,512]{1,0:T(8,128)} %copy-done.9, f32[16,512]{1,0:T(8,128)} %copy-done.8, f32[16,512]{1,0:T(8,128)} %d_ref.7), custom_call_target="tpu_custom_call" | custom-call | flops 10000000 | bytes 1000000 | tf_op jit(solution)/shard_map/group/pallas_call | solution.py:68
  22.4 9.5 %collective-permute-start.10 = (f32[16,512]{1,0:T(8,128)}, f32[16,512]{1,0:T(8,128)S(1)}, u32[]{:S(2)}, u32[]{:S(2)}) collective-permute-start(f32[16,512]{1,0:T(8,128)} %get-tuple-element.14), channel_id=1, source_target_pairs={{0,224},{8,232},{16,240},{24,248},{1,225},{9,233},{17,241},{25,249... | collective-permute-start | bytes 98312 | tf_op jit(solution)/shard_map/ppermute | solution.py:243
  31.9 1.3 %collective-permute-start.9 = (f32[16,512]{1,0:T(8,128)}, f32[16,512]{1,0:T(8,128)S(1)}, u32[]{:S(2)}, u32[]{:S(2)}) collective-permute-start(f32[16,512]{1,0:T(8,128)} %get-tuple-element.14), channel_id=1, source_target_pairs={{0,192},{8,200},{16,208},{24,216},{32,224},{40,232},{48,240},{56,2... | collective-permute-start | bytes 98312 | tf_op jit(solution)/shard_map/ppermute | solution.py:243
  33.2 1.3 %collective-permute-start.8 = (f32[16,512]{1,0:T(8,128)}, f32[16,512]{1,0:T(8,128)S(1)}, u32[]{:S(2)}, u32[]{:S(2)}) collective-permute-start(f32[16,512]{1,0:T(8,128)} %get-tuple-element.14), channel_id=1, source_target_pairs={{0,160},{8,168},{16,176},{24,184},{32,192},{40,200},{48,208},{56,2... | collective-permute-start | bytes 98312 | tf_op jit(solution)/shard_map/ppermute | solution.py:243
  34.5 2.0 %collective-permute-start.7 = (f32[16,512]{1,0:T(8,128)}, f32[16,512]{1,0:T(8,128)S(1)}, u32[]{:S(2)}, u32[]{:S(2)}) collective-permute-start(f32[16,512]{1,0:T(8,128)} %get-tuple-element.14), channel_id=1, source_target_pairs={{0,128},{8,136},{16,144},{24,152},{32,160},{40,168},{48,176},{56,1... | collective-permute-start | bytes 98312 | tf_op jit(solution)/shard_map/ppermute | solution.py:243
  36.5 4.5 %collective-permute-start.6 = (f32[16,512]{1,0:T(8,128)}, f32[16,512]{1,0:T(8,128)S(1)}, u32[]{:S(2)}, u32[]{:S(2)}) collective-permute-start(f32[16,512]{1,0:T(8,128)} %get-tuple-element.14), channel_id=1, source_target_pairs={{0,96},{8,104},{16,112},{24,120},{32,128},{40,136},{48,144},{56,15... | collective-permute-start | bytes 98312 | tf_op jit(solution)/shard_map/ppermute | solution.py:243
  41.0 0.0 collective-permute-done.10.rest_6_
  41.0 0.0 copy-start.1
  41.0 1.3 %collective-permute-start.5 = (f32[16,512]{1,0:T(8,128)}, f32[16,512]{1,0:T(8,128)S(1)}, u32[]{:S(2)}, u32[]{:S(2)}) collective-permute-start(f32[16,512]{1,0:T(8,128)} %get-tuple-element.14), channel_id=1, source_target_pairs={{0,64},{8,72},{16,80},{24,88},{32,96},{40,104},{48,112},{56,120},{... | collective-permute-start | bytes 98312 | tf_op jit(solution)/shard_map/ppermute | solution.py:243
  42.3 0.0 collective-permute-done.9.rest_5_
  42.4 0.0 copy-start.2
  42.4 3.1 %collective-permute-start.4 = (f32[16,512]{1,0:T(8,128)}, f32[16,512]{1,0:T(8,128)S(1)}, u32[]{:S(2)}, u32[]{:S(2)}) collective-permute-start(f32[16,512]{1,0:T(8,128)} %get-tuple-element.14), channel_id=1, source_target_pairs={{0,32},{8,40},{16,48},{24,56},{32,64},{40,72},{48,80},{56,88},{64,... | collective-permute-start | bytes 98312 | tf_op jit(solution)/shard_map/ppermute | solution.py:243
  45.5 3.8 %local.1.local_ref = f32[128,512]{1,0:T(8,128)} custom-call(f32[128,512]{1,0:T(8,128)} %get-tuple-element.11.mixed_ref, f32[16,512]{1,0:T(8,128)} %res_ref.3, f32[16,512]{1,0:T(8,128)} %d_ref.7, f32[1,512]{1,0:T(1,128)} %bitcast.1), custom_call_target="tpu_custom_call" | custom-call | flops 1000000000 | bytes 1000000 | tf_op jit(solution)/shard_map/local/pallas_call | solution.py:68
  49.3 0.0 collective-permute-done.8.rest_4_
  49.3 0.0 collective-permute-done.7.rest_3_
  49.3 0.0 copy-start.4
  49.3 0.0 collective-permute-done.6.rest_2_
  49.3 0.0 copy-start.5
  49.4 0.0 collective-permute-done.5.rest_1_
  49.4 0.0 copy-start.6
  49.4 0.0 collective-permute-done.4.rest_0_
  49.4 0.0 copy-start.7
  49.4 0.0 copy-done.1
  49.4 0.0 copy-done.2
  49.4 0.5 copy-done.3
  49.9 0.0 copy-done.4
  49.9 0.0 copy-done.5
  49.9 0.0 copy-done.6
  50.0 0.0 copy-done.7
  50.0 3.4 %gate.1.gated_ref = f32[128,512]{1,0:T(8,128)} custom-call(f32[128,512]{1,0:T(8,128)} %get-tuple-element.10.query_ref, f32[128,512]{1,0:T(8,128)} %local.1.local_ref, f32[16,512]{1,0:T(8,128)} %get-tuple-element.13.before_ref, f32[16,512]{1,0:T(8,128)} %res_ref.3, f32[16,512]{1,0:T(8,128)} %d_ref.7, f32[16,512]{1,0:T(8,128)} %copy-done.7, ...), custom_call_target="tpu_custom_call" | custom-call | flops 10000000 | bytes 1000000 | tf_op jit(solution)/shard_map/gate/pallas_call | solution.py:68
  53.4 8.1 %project.1 = bf16[8,128,1024]{2,1,0:T(8,128)(2,1)} custom-call(f32[128,512]{1,0:T(8,128)} %gate.1.gated_ref, bf16[512,8192]{1,0:T(8,128)(2,1)} %w_ref.3), custom_call_target="tpu_custom_call" | custom-call | tf_op jit(solution)/shard_map/project/pallas_call | solution.py:153
  61.5 31.7 %all_to_all.5 = bf16[8,128,1024]{2,1,0:T(8,128)(2,1)S(1)} all-to-all(bf16[8,128,1024]{2,1,0:T(8,128)(2,1)} %project.1), channel_id=1, replica_groups=mesh['ctx'=32,'ch'=8] {'ch'}, dimensions={0} | all-to-all | bytes 4194304 | tf_op jit(solution)/shard_map/all_to_all | solution.py:205
  93.2 1.1 %reduce_sum.12 = bf16[128,1024]{1,0:T(8,128)(2,1)} reduce(bf16[8,128,1024]{2,1,0:T(8,128)(2,1)S(1)} %all_to_all.5, bf16[]{:T(256)} %constant.2.clone.1), dimensions={0}, to_apply=%region_0.0 | reduce | flops 917504 | bytes 2359298 | tf_op jit(solution)/shard_map/reduce_sum | solution.py:206
  (4 shorter events, 0.0 us)
Async XLA Ops:
  1.4 6.7 %collective-permute-start = (f32[48,512]{1,0:T(8,128)}, f32[48,512]{1,0:T(8,128)S(1)}, u32[]{:S(2)}, u32[]{:S(2)}) collective-permute-start(f32[48,512]{1,0:T(8,128)} %edge.1), channel_id=1, source_target_pairs={{0,8},{8,16},{16,24},{24,32},{32,40},{40,48},{48,56},{56,64},{64,7... | collective-permute-start | bytes 294920 | tf_op jit(solution)/shard_map/ppermute | solution.py:215
  8.1 0.6 copy-start
  11.9 4.8 %collective-permute-start.3 = (f32[16,512]{1,0:T(8,128)}, f32[16,512]{1,0:T(8,128)S(1)}, u32[]{:S(2)}, u32[]{:S(2)}) collective-permute-start(f32[16,512]{1,0:T(8,128)} %get-tuple-element.12.own_ref), channel_id=1, source_target_pairs={{0,24},{8,0},{16,8},{24,16},{32,56},{40,32},{48,40},{56,48},{64,88... | collective-permute-start | bytes 98312 | tf_op jit(solution)/shard_map/ppermute | solution.py:225
  11.9 5.7 %collective-permute-start.2 = (f32[16,512]{1,0:T(8,128)}, f32[16,512]{1,0:T(8,128)S(1)}, u32[]{:S(2)}, u32[]{:S(2)}) collective-permute-start(f32[16,512]{1,0:T(8,128)} %get-tuple-element.12.own_ref), channel_id=1, source_target_pairs={{0,16},{8,24},{16,0},{24,8},{32,48},{40,56},{48,32},{56,40},{64,80... | collective-permute-start | bytes 98312 | tf_op jit(solution)/shard_map/ppermute | solution.py:225
  14.9 4.1 %collective-permute-start.1 = (f32[16,512]{1,0:T(8,128)}, f32[16,512]{1,0:T(8,128)S(1)}, u32[]{:S(2)}, u32[]{:S(2)}) collective-permute-start(f32[16,512]{1,0:T(8,128)} %get-tuple-element.12.own_ref), channel_id=1, source_target_pairs={{0,8},{8,16},{16,24},{24,0},{32,40},{40,48},{48,56},{56,32},{64,72... | collective-permute-start | bytes 98312 | tf_op jit(solution)/shard_map/ppermute | solution.py:225
  16.7 2.3 %copy-start.8 = (f32[16,512]{1,0:T(8,128)}, f32[16,512]{1,0:T(8,128)S(1)}, u32[]{:S(2)}) copy-start(f32[16,512]{1,0:T(8,128)S(1)} %collective-permute-done.3.r3_ref) | copy-start | bytes 98308
  17.7 1.4 %copy-start.9 = (f32[16,512]{1,0:T(8,128)}, f32[16,512]{1,0:T(8,128)S(1)}, u32[]{:S(2)}) copy-start(f32[16,512]{1,0:T(8,128)S(1)} %collective-permute-done.2.r2_ref) | copy-start | bytes 98308
  19.0 0.6 copy-start.10
  22.4 18.6 %collective-permute-start.10 = (f32[16,512]{1,0:T(8,128)}, f32[16,512]{1,0:T(8,128)S(1)}, u32[]{:S(2)}, u32[]{:S(2)}) collective-permute-start(f32[16,512]{1,0:T(8,128)} %get-tuple-element.14), channel_id=1, source_target_pairs={{0,224},{8,232},{16,240},{24,248},{1,225},{9,233},{17,241},{25,249... | collective-permute-start | bytes 98312 | tf_op jit(solution)/shard_map/ppermute | solution.py:243
  31.9 10.4 %collective-permute-start.9 = (f32[16,512]{1,0:T(8,128)}, f32[16,512]{1,0:T(8,128)S(1)}, u32[]{:S(2)}, u32[]{:S(2)}) collective-permute-start(f32[16,512]{1,0:T(8,128)} %get-tuple-element.14), channel_id=1, source_target_pairs={{0,192},{8,200},{16,208},{24,216},{32,224},{40,232},{48,240},{56,2... | collective-permute-start | bytes 98312 | tf_op jit(solution)/shard_map/ppermute | solution.py:243
  33.2 16.1 %collective-permute-start.8 = (f32[16,512]{1,0:T(8,128)}, f32[16,512]{1,0:T(8,128)S(1)}, u32[]{:S(2)}, u32[]{:S(2)}) collective-permute-start(f32[16,512]{1,0:T(8,128)} %get-tuple-element.14), channel_id=1, source_target_pairs={{0,160},{8,168},{16,176},{24,184},{32,192},{40,200},{48,208},{56,2... | collective-permute-start | bytes 98312 | tf_op jit(solution)/shard_map/ppermute | solution.py:243
  34.5 14.8 %collective-permute-start.7 = (f32[16,512]{1,0:T(8,128)}, f32[16,512]{1,0:T(8,128)S(1)}, u32[]{:S(2)}, u32[]{:S(2)}) collective-permute-start(f32[16,512]{1,0:T(8,128)} %get-tuple-element.14), channel_id=1, source_target_pairs={{0,128},{8,136},{16,144},{24,152},{32,160},{40,168},{48,176},{56,1... | collective-permute-start | bytes 98312 | tf_op jit(solution)/shard_map/ppermute | solution.py:243
  36.5 12.8 %collective-permute-start.6 = (f32[16,512]{1,0:T(8,128)}, f32[16,512]{1,0:T(8,128)S(1)}, u32[]{:S(2)}, u32[]{:S(2)}) collective-permute-start(f32[16,512]{1,0:T(8,128)} %get-tuple-element.14), channel_id=1, source_target_pairs={{0,96},{8,104},{16,112},{24,120},{32,128},{40,136},{48,144},{56,15... | collective-permute-start | bytes 98312 | tf_op jit(solution)/shard_map/ppermute | solution.py:243
  41.0 8.4 %copy-start.1 = (f32[16,512]{1,0:T(8,128)}, f32[16,512]{1,0:T(8,128)S(1)}, u32[]{:S(2)}) copy-start(f32[16,512]{1,0:T(8,128)S(1)} %collective-permute-done.10.rest_6_) | copy-start | bytes 98308
  41.0 8.3 %collective-permute-start.5 = (f32[16,512]{1,0:T(8,128)}, f32[16,512]{1,0:T(8,128)S(1)}, u32[]{:S(2)}, u32[]{:S(2)}) collective-permute-start(f32[16,512]{1,0:T(8,128)} %get-tuple-element.14), channel_id=1, source_target_pairs={{0,64},{8,72},{16,80},{24,88},{32,96},{40,104},{48,112},{56,120},{... | collective-permute-start | bytes 98312 | tf_op jit(solution)/shard_map/ppermute | solution.py:243
  42.4 7.1 %copy-start.2 = (f32[16,512]{1,0:T(8,128)}, f32[16,512]{1,0:T(8,128)S(1)}, u32[]{:S(2)}) copy-start(f32[16,512]{1,0:T(8,128)S(1)} %collective-permute-done.9.rest_5_) | copy-start | bytes 98308
  42.4 7.0 %collective-permute-start.4 = (f32[16,512]{1,0:T(8,128)}, f32[16,512]{1,0:T(8,128)S(1)}, u32[]{:S(2)}, u32[]{:S(2)}) collective-permute-start(f32[16,512]{1,0:T(8,128)} %get-tuple-element.14), channel_id=1, source_target_pairs={{0,32},{8,40},{16,48},{24,56},{32,64},{40,72},{48,80},{56,88},{64,... | collective-permute-start | bytes 98312 | tf_op jit(solution)/shard_map/ppermute | solution.py:243
  49.3 0.6 copy-start.3
  49.3 0.6 copy-start.4
  49.3 0.6 copy-start.5
  49.4 0.6 copy-start.6
  49.4 0.6 copy-start.7
